TPU v7x, 128 devices: a whole 4x4x4 slice. The times are simulated.
128 devices in a mesh: prow: 8 (over y_lo, z), pcol: 16 (over x, y_hi, core).
Axes of the slice: x: 4, y: 4 (y_hi: 2, y_lo: 2; y = y_hi * 2 + y_lo), z: 4, core: 2. Of those that a mesh axis runs over, the one named last changes fastest.
Arguments:
- anc_inverse: float32 [4096, 4096], P('pcol', 'prow')
- pattern_one: int32 [16, 8], replicated, may hold values from 0 to 15, as said below
- parents: int32 [16], replicated, may hold values from 0 to 15, as said below
- low_one: float32 [16, 2048, 256], P('pcol', 'prow'), may hold values from -2 to 2
- pivot_one: float32 [16, 256, 256], P('pcol'), may hold values from -4 to 4
- low_two: float32 [16, 2048, 256], P('pcol', 'prow'), may hold values from -2 to 2
- second_scaled_factor: float32 [16, 256, 256], P('pcol'), may hold values from -2 to 2
- second_pivot_inverse: float32 [16, 256, 256], P('pcol'), may hold values from -4 to 4
Outputs:
- column_one: float32 [16, 4096, 256], P('prow', 'pcol')
- diag_one: float32 [16, 256, 256], P('pcol')
- column_two: float32 [16, 4096, 256], P('prow', 'pcol')
- second_parent_inverse: float32 [16, 256, 256], P('pcol')
- second_diagonal_inverse: float32 [16, 256, 256], P('pcol')
Inputs may be any that keep to these rules, and one draw needn't show every extreme that they name: `pattern_one`: entry r of each row names an ancestor of process row r: it lies in r * 2 to r * 2 + 1; for each r, every ancestor of that range is entry r of exactly 8 rows. `parents`: every first-level supernode is the parent of exactly one second-level supernode.
All inputs are finite; a program needn't handle non-finite values.
Results may differ from a plain program's by a relative error of at most 0.000073.
Values sent between devices are 32-bit elements; how exact they have to be, the bound alone decides.
No kernel may reach another device: no remote copies, remote signals or barrier semaphores. Data moves between devices by JAX's collectives and lax.ppermute only.
A program may use at most 128 MiB of HBM per device.

v0:
```python
import jax
import jax.numpy as jnp
from jax import lax
from jax.sharding import PartitionSpec as P


def in_one_piece(arrays, axis, dim, along):
    widths = [a.shape[along] for a in arrays]
    both = jnp.concatenate(arrays, axis=along)
    result = lax.all_gather(both, axis, axis=dim, tiled=True)
    return tuple(jnp.split(result, [sum(widths[:k]) for k in range(1, len(widths))], axis=along))


def sent_to_all(x, axis):
    copies = jnp.broadcast_to(x, (lax.axis_size(axis), *x.shape))
    return lax.all_to_all(copies, axis, split_axis=0, concat_axis=0, tiled=True)


def over_copies(x, axis):
    return sent_to_all(x, axis).sum(axis=0)


def side_by_side(arrays, axis, dim, along):
    both = jnp.concatenate(arrays, axis=along)
    result, at, outs = (lax.psum_scatter(both, axis, scatter_dimension=dim, tiled=True), 0, [])
    for a in arrays:
        outs.append(lax.slice_in_dim(result, at, at + a.shape[along], axis=along))
        at += a.shape[along]
    return tuple(outs)


def together(arrays, axis):
    line, at, outs = (jnp.concatenate([a.reshape(-1) for a in arrays]), 0, [])
    subtotal = over_copies(line, axis)
    for a in arrays:
        outs.append(subtotal[at : at + a.size].reshape(a.shape))
        at += a.size
    return tuple(outs)


def batched(left, right):
    return jnp.einsum("kab,kbd->kad", left, right, precision=lax.Precision.HIGHEST)


def batched_left_t(left, right):
    return jnp.einsum("kba,kbd->kad", left, right, precision=lax.Precision.HIGHEST)


def pick_rows(hit_mask, count):
    total = hit_mask.shape[0]
    keys = jnp.where(hit_mask, 0, total).astype(jnp.int32) + jnp.arange(total, dtype=jnp.int32)
    chosen_rows = jnp.argsort(keys)[:count]
    valid = jnp.take(hit_mask, chosen_rows, axis=0).astype(jnp.float32)[:, None, None]
    return (chosen_rows, valid)


def body(
    anc_inverse,
    pattern_one,
    parents,
    low_one,
    pivot_one,
    low_two,
    second_scaled_factor,
    second_pivot_inverse,
):
    my_row = lax.axis_index("prow")
    my_col = lax.axis_index("pcol")
    row_count = lax.axis_size("prow")
    col_count = lax.axis_size("pcol")
    per_row_anc = col_count // row_count
    supernode_block_width = pivot_one.shape[1]
    per_col_one = pivot_one.shape[0]
    per_col_two = second_scaled_factor.shape[0]
    owned = anc_inverse.shape[1] // supernode_block_width
    zblocks = anc_inverse.reshape(supernode_block_width, owned, supernode_block_width).transpose(
        1, 0, 2
    )
    lowall = lax.all_gather(low_one, "pcol", axis=0, tiled=True)
    total_one = lowall.shape[0]
    owned_slot_list = lax.dynamic_index_in_dim(pattern_one, my_row, 1, keepdims=False)
    chosen = jnp.take(zblocks, owned_slot_list - my_row * owned, axis=0)
    first_terms = batched(chosen, lowall)
    lowsec, topall = in_one_piece((low_two, second_scaled_factor), "pcol", 0, 1)
    total_two = lowsec.shape[0]
    pattern_two = jnp.take(pattern_one, parents, axis=0)
    my_slots_two = lax.dynamic_index_in_dim(pattern_two, my_row, 1, keepdims=False)
    chosen_two = jnp.take(zblocks, my_slots_two - my_row * owned, axis=0)
    first_full = -lax.psum(first_terms, "prow")
    share = total_two // row_count
    start = my_row * share
    parents_share = lax.dynamic_slice_in_dim(parents, start, share, 0)
    tops_share = lax.dynamic_slice_in_dim(topall, start, share, 0)
    carried = batched(jnp.take(first_full, parents_share, axis=0), tops_share)
    base_terms = batched(chosen_two, lowsec)
    updated = lax.dynamic_slice_in_dim(base_terms, start, share, 0) + carried
    second_terms = lax.dynamic_update_slice_in_dim(base_terms, updated, start, 0)
    second_full = -lax.psum(second_terms, "prow")
    rows_one, valid_one = pick_rows(owned_slot_list == my_col, total_one // per_row_anc)
    pivot_small = valid_one * batched_left_t(
        jnp.take(lowall, rows_one, axis=0), jnp.take(first_full, rows_one, axis=0)
    )
    pivot_terms = jnp.zeros_like(first_full).at[rows_one].add(pivot_small)
    pivot_part = lax.psum_scatter(pivot_terms, "pcol", scatter_dimension=0, tiled=True)
    pivot_sum = over_copies(pivot_part, "prow")
    diag_one = pivot_one - pivot_sum
    count_one = first_full.shape[0] // row_count
    column_one = lax.dynamic_slice_in_dim(first_full, my_row * count_one, count_one, 0)
    second_level_count = second_full.shape[0] // row_count
    column_two = lax.dynamic_slice_in_dim(
        second_full, my_row * second_level_count, second_level_count, 0
    )
    rows_two, valid_two = pick_rows(my_slots_two == my_col, total_two // per_row_anc)
    lows_picked = jnp.take(lowsec, rows_two, axis=0)
    parent_picked = jnp.take(first_full, jnp.take(parents, rows_two, axis=0), axis=0)
    cross_small = valid_two * batched_left_t(parent_picked, lows_picked)
    diag_small = valid_two * batched_left_t(lows_picked, jnp.take(second_full, rows_two, axis=0))
    local_parent = parents - my_col * per_col_one
    own_parent = (local_parent >= 0) & (local_parent < per_col_one)
    rows_own, valid_own = pick_rows(own_parent, per_col_two)
    valid_own = valid_own * (my_row == 0).astype(jnp.float32)
    local_picked = jnp.clip(jnp.take(local_parent, rows_own, axis=0), 0, per_col_one - 1)
    picked = jnp.take(diag_one, local_picked, axis=0)
    own_small = valid_own * batched(picked, jnp.take(topall, rows_own, axis=0))
    cross_terms = (
        jnp.zeros_like(second_full).at[rows_two].add(cross_small).at[rows_own].add(own_small)
    )
    diag_terms = jnp.zeros_like(second_full).at[rows_two].add(diag_small)
    part_cross, part_diag = side_by_side((cross_terms, diag_terms), "pcol", 0, 1)
    sum_cross, sum_diag = together((part_cross, part_diag), "prow")
    second_parent_inverse = -sum_cross
    second_diagonal_inverse = (
        second_pivot_inverse
        - batched_left_t(second_scaled_factor, second_parent_inverse)
        - sum_diag
    )
    return (column_one, diag_one, column_two, second_parent_inverse, second_diagonal_inverse)


def solution(mesh):
    placed = (
        P("pcol", "prow"),
        P(),
        P(),
        P("pcol", "prow", None),
        P("pcol", None, None),
        P("pcol", "prow", None),
        P("pcol", None, None),
        P("pcol", None, None),
    )
    return jax.shard_map(
        body,
        mesh=mesh,
        in_specs=placed,
        out_specs=(
            P("prow", "pcol", None),
            P("pcol", None, None),
            P("prow", "pcol", None),
            P("pcol", None, None),
            P("pcol", None, None),
        ),
        check_vma=False,
    )
```

profile of v0, /device:TPU:1, one launch (start us, length us, event | category | flops | bytes accessed | tf_op | source)
XLA Modules:
  0.0 673.7 jit_solution(4868192869001686954)
XLA Ops:
  11.0 2.8 gather_fusion.3
  13.8 56.2 %all-gather.3.cloned.1.call-done = f32[16,256,256]{2,1,0:T(8,128)} async-done(((f32[1,256,256]{2,1,0:T(8,128)}), f32[16,256,256]{2,1,0:T(8,128)}) %all-gather.3.cloned.1.call-update) | async-done | bytes 4194320 | tf_op jit(solution)/shard_map/all_gather | solution.py:79
  70.0 9.7 %fusion.2 = f32[16,256,256]{2,1,0:T(8,128)} fusion(f32[16,256,256]{2,1,0:T(8,128)} %all-gather.3.cloned.1.call-done, f32[16,256,256]{2,1,0:T(8,128)} %gather_fusion.3, pred[16]{0:T(512)(128)(4,1)S(1)} %compare_and_fusion.4), kind=kOutput, calls=%fused_computation.18 | convolution fusion | flops 3222274048 | bytes 12582928 | tf_op jit(solution)/shard_map/kab,kbd->kad/dot_general | solution.py:42
  83.8 4.2 gather_fusion.5
  88.0 95.9 %all-reduce.3.cloned.1.call-done = f32[16,256,256]{2,1,0:T(8,128)} async-done(((f32[16,256,256]{2,1,0:T(8,128)}), f32[16,256,256]{2,1,0:T(8,128)}) %all-reduce.3.cloned.1.call-update) | async-done | bytes 4194320 | tf_op jit(solution)/shard_map/psum | solution.py:89
  183.9 4.5 neg.15
  188.4 4.2 gather_fusion.6
  192.6 6.1 fusion.17
  201.1 4.4 scatter_fusion
  207.0 2.7 gather_fusion.7
  209.8 2.8 gather_fusion.1
  212.6 46.1 %all-gather.5.cloned.1.call-done = f32[16,512,256]{2,1,0:T(8,128)} async-done(((f32[1,512,256]{2,1,0:T(8,128)}), f32[16,512,256]{2,1,0:T(8,128)}) %all-gather.5.cloned.1.call-update) | async-done | bytes 8388624 | tf_op jit(solution)/shard_map/all_gather | solution.py:10
  258.7 6.4 fusion.67
  267.2 5.6 fusion
  275.4 63.5 %reduce-scatter.3.cloned.1.call-done = f32[1,256,256]{2,1,0:T(8,128)} async-done(((f32[16,256,256]{2,1,0:T(8,128)}), f32[1,256,256]{2,1,0:T(8,128)}) %reduce-scatter.3.cloned.1.call-update) | async-done | bytes 262160 | tf_op jit(solution)/shard_map/reduce_scatter | solution.py:104
  341.5 4.4 all-to-all-start
  353.0 4.2 gather_fusion.9
  357.2 2.9 gather_fusion.10
  360.1 6.7 %fusion.22 = f32[8,256,256]{2,1,0:T(8,128)} fusion(f32[8,256,256]{2,1,0:T(8,128)S(1)} %gather_fusion.10, f32[8,256,256]{2,1,0:T(8,128)} %gather_fusion.9, f32[8]{0:T(128)S(1)} %get-tuple-element.106, pred[8]{0:T(512)(128)(4,1)S(1)} %get-tuple-element.93, pred[8]{0:T(512)(128)(4,1)S(1)} %get-tuple-element.91), kind=kOutput, calls=%fused_computation.34 | convolution fusion | flops 1612185600 | bytes 6291504 | tf_op jit(solution)/shard_map/kba,kbd->kad/dot_general | solution.py:46
  369.3 5.3 scatter_fusion.1
  374.6 90.7 %all-reduce.5.cloned.1.call-done = f32[16,256,256]{2,1,0:T(8,128)} async-done(((f32[16,256,256]{2,1,0:T(8,128)}), f32[16,256,256]{2,1,0:T(8,128)}) %all-reduce.5.cloned.1.call-update) | async-done | bytes 4194320 | tf_op jit(solution)/shard_map/psum | solution.py:98
  465.3 4.5 neg.16
  469.7 4.2 gather_fusion.11
  474.0 6.7 fusion.27
  483.0 4.4 scatter_fusion.2
  489.2 2.8 fusion.36
  492.0 7.4 %pad_maximum_fusion = f32[16,512,256]{2,1,0:T(8,128)} fusion(f32[16,256,256]{2,1,0:T(8,128)} %scatter_fusion.2, f32[16,256,256]{2,1,0:T(8,128)} %fusion.36), kind=kLoop, calls=%fused_computation.15 | loop fusion | flops 2097152 | bytes 16777216 | tf_op jit(solution)/shard_map/concatenate | solution.py:24
  499.5 100.2 %reduce-scatter.5.cloned.1.call-done = f32[1,512,256]{2,1,0:T(8,128)} async-done(((f32[16,512,256]{2,1,0:T(8,128)}), f32[1,512,256]{2,1,0:T(8,128)}) %reduce-scatter.5.cloned.1.call-update) | async-done | bytes 524304 | tf_op jit(solution)/shard_map/reduce_scatter | solution.py:25
  601.1 4.1 broadcast_in_dim.125
  605.2 4.9 all-to-all-start.1
  614.0 44.8 %all-to-all-done.1 = f32[8,1,131072]{2,1,0:T(1,128)} async-done(((f32[8,1,131072]{2,1,0:T(1,128)}), f32[8,1,131072]{2,1,0:T(1,128)}, u32[]{:S(2)}, u32[]{:S(2)}) %all-to-all-start.1) | async-done | bytes 4194336 | tf_op jit(solution)/shard_map/all_to_all | solution.py:16
  658.8 5.2 reduce_sum.22
  (96 shorter events, 39.1 us)
Async XLA Ops:
  7.2 62.9 %all-gather.3.cloned.1.call-start = ((), (), s32[]{:S(2)}) async-start(), calls=%async_computation.4 | async-start | bytes 4456448 | tf_op jit(solution)/shard_map/all_gather | solution.py:79
  7.9 176.0 %all-reduce.3.cloned.1.call-start = ((), (), s32[]{:S(2)}) async-start(), calls=%async_computation.5 | async-start | bytes 8388608 | tf_op jit(solution)/shard_map/psum | solution.py:89
  79.7 0.9 copy-start.6
  79.7 1.0 copy-start.9
  79.8 178.9 %all-gather.5.cloned.1.call-start = ((), (), s32[]{:S(2)}) async-start(), calls=%async_computation.7 | async-start | bytes 8912896 | tf_op jit(solution)/shard_map/all_gather | solution.py:10
  81.6 257.4 %reduce-scatter.3.cloned.1.call-start = ((), (), s32[]{:S(2)}) async-start(), calls=%async_computation.6 | async-start | bytes 4456448 | tf_op jit(solution)/shard_map/reduce_scatter | solution.py:104
  201.1 4.9 copy-start
  205.5 259.8 %all-reduce.5.cloned.1.call-start = ((), (), s32[]{:S(2)}) async-start(), calls=%async_computation.8 | async-start | bytes 8388608 | tf_op jit(solution)/shard_map/psum | solution.py:98
  258.7 7.2 %copy-start.1 = (f32[16,512,256]{2,1,0:T(8,128)S(1)}, f32[16,512,256]{2,1,0:T(8,128)}, u32[]{:S(2)}) copy-start(f32[16,512,256]{2,1,0:T(8,128)} %all-gather.5.cloned.1.call-done) | copy-start | bytes 25165828
  258.7 8.5 %copy-start.2 = (f32[16,256,256]{2,1,0:T(8,128)S(1)}, f32[16,256,256]{2,1,0:T(8,128)}, u32[]{:S(2)}) copy-start(f32[16,256,256]{2,1,0:T(8,128)} %gather_fusion.7) | copy-start | bytes 12582916
  267.2 5.6 copy-start.4
  275.4 76.9 %copy-start.10 = (s32[3]{0:T(128)S(1)}, s32[3]{0:T(128)}, u32[]{:S(2)}) copy-start(s32[3]{0:T(128)} %constant.173.clone.1) | copy-start | bytes 40
  341.5 145.9 %all-to-all-start = ((f32[8,1,256,256]{3,2,1,0:T(8,128)}), f32[8,1,256,256]{3,2,1,0:T(8,128)}, u32[]{:S(2)}, u32[]{:S(2)}) async-start(f32[8,1,256,256]{3,2,1,0:T(8,128)} %broadcast_in_dim.110), calls=%async_computation.1 | async-start | bytes 4194304 | tf_op jit(solution)/shard_map/all_to_all | solution.py:16
  345.9 253.8 %reduce-scatter.5.cloned.1.call-start = ((), (), s32[]{:S(2)}) async-start(), calls=%async_computation.9 | async-start | bytes 8912896 | tf_op jit(solution)/shard_map/reduce_scatter | solution.py:25
  480.7 2.4 copy-start.3
  483.0 6.1 copy-start.7
  489.2 10.2 %copy-start.5 = (f32[1,256,256]{2,1,0:T(8,128)}, f32[1,256,256]{2,1,0:T(8,128)S(1)}, u32[]{:S(2)}) copy-start(f32[1,256,256]{2,1,0:T(8,128)S(1)} %bitcast_subtract_fusion) | copy-start | bytes 786436
  605.2 4.9 copy-start.8
  605.2 53.5 %all-to-all-start.1 = ((f32[8,1,131072]{2,1,0:T(1,128)}), f32[8,1,131072]{2,1,0:T(1,128)}, u32[]{:S(2)}, u32[]{:S(2)}) async-start(f32[8,1,131072]{2,1,0:T(1,128)} %broadcast_in_dim.125), calls=%async_computation.3 | async-start | bytes 8388608 | tf_op jit(solution)/shard_map/all_to_all | solution.py:16
Sparse Core Ops, SparseCore 0:
  10.4 59.5 all-gather.2
  79.9 103.9 all-reduce.2
  186.9 71.8 all-gather.4
  262.6 76.3 reduce-scatter.2
  341.5 123.7 all-reduce.4
  499.6 100.0 reduce-scatter.4
where the time goes:
time: 683 us; the launch traced here: 674 us
  waiting for transfers between devices  498 us (73%)
  local copies, waits for them, and re-layouts  64.3 us (9%)
  other arithmetic  44.5 us (7%)
  matrix products  40.7 us (6%)
  between operations  16 us (2%)
  starting transfers between devices  9.97 us (1%)
    reduce_scatter x1, waiting for transfers between devices, side_by_side(): lax.psum_scatter(both, axis, scatter_dimension=dim, tiled=True)  100 us
    psum x1, waiting for transfers between devices, body(): first_full = -lax.psum(first_terms, 'prow')  95.9 us
    psum x1, waiting for transfers between devices, body(): second_full = -lax.psum(second_terms, 'prow')  90.7 us
    reduce_scatter x1, waiting for transfers between devices, body(): lax.psum_scatter(pivot_terms, 'pcol', scatter_dimension=0, tiled=True)  63.5 us
    all_gather x1, waiting for transfers between devices, body(): lowall = lax.all_gather(low_one, 'pcol', axis=0, tiled=True)  56.2 us
    all_gather x1, waiting for transfers between devices, in_one_piece(): result = lax.all_gather(both, axis, axis=dim, tiled=True)  46.1 us
    all_to_all x2, waiting for transfers between devices, sent_to_all(): return lax.all_to_all(copies, axis, split_axis=0, concat_axis=0, tiled=True)  44.8 us
    dot_general x4, matrix products, batched(): jnp.einsum('kab,kbd->kad', left, right, precision=lax.Precision.HIGHEST)  20.6 us
  transfers between devices with their start and end apart: 8, of which 7 were waited for; matrix products, arithmetic and copies ran while one was open for 17% of the time, Pallas kernels for 0%

commit v1 on v0

--- a/solution.py
+++ b/solution.py
@@ -2,6 +2,11 @@
 import jax.numpy as jnp
 from jax import lax
 from jax.sharding import PartitionSpec as P
+
+
+def gather_over(x, name, dim):
+    repeated = jnp.stack([x] * lax.axis_size(name))
+    return jnp.concatenate(lax.all_to_all(repeated, name, 0, 0), axis=dim)
 
 
 def in_one_piece(arrays, axis, dim, along):
@@ -76,7 +81,7 @@
     zblocks = anc_inverse.reshape(supernode_block_width, owned, supernode_block_width).transpose(
         1, 0, 2
     )
-    lowall = lax.all_gather(low_one, "pcol", axis=0, tiled=True)
+    lowall = gather_over(low_one, "pcol", 0)
     total_one = lowall.shape[0]
     owned_slot_list = lax.dynamic_index_in_dim(pattern_one, my_row, 1, keepdims=False)
     chosen = jnp.take(zblocks, owned_slot_list - my_row * owned, axis=0)

time: 683 us -> 614 us (0.90)
  waiting for transfers between devices: 498 us -> 407 us
  starting transfers between devices: 9.97 us -> 33.1 us
    psum x1, waiting for transfers between devices: 90.7 us -> 23.9 us  [body(): second_full = -lax.psum(second_terms, 'prow')]
    all_gather x1 -> x0, waiting for transfers between devices: 56.2 us -> none  [body(): lowall = lax.all_gather(low_one, 'pcol', axis=0, tiled=True)]
    all_to_all x0 -> x1, waiting for transfers between devices: none -> 49.2 us  [gather_over(): return jnp.concatenate(lax.all_to_all(repeated, name, 0, 0), axis=dim)]
    all_gather x1, waiting for transfers between devices: 46.1 us -> 0.03 us  [in_one_piece(): result = lax.all_gather(both, axis, axis=dim, tiled=True)]
    psum x1, waiting for transfers between devices: 95.9 us -> 133 us  [body(): first_full = -lax.psum(first_terms, 'prow')]
    reduce_scatter x1, starting transfers between devices: 0.04 us -> 10.9 us  [side_by_side(): lax.psum_scatter(both, axis, scatter_dimension=dim, tiled=True)]
    all_to_all x0 -> x1, starting transfers between devices: none -> 8.58 us  [gather_over(): return jnp.concatenate(lax.all_to_all(repeated, name, 0, 0), axis=dim)]
  transfers between devices with their start and end apart: 8 -> 8, of which waited for: 7 -> 7; matrix products, arithmetic and copies ran while one was open for 17% -> 15% of each run, Pallas kernels for 0% -> 0%
where the time goes in v1:
time: 614 us; the launch traced here: 609 us
  waiting for transfers between devices  407 us (66%)
  local copies, waits for them, and re-layouts  66.8 us (11%)
  other arithmetic  43.6 us (7%)
  matrix products  40.8 us (7%)
  starting transfers between devices  33.1 us (5%)
  between operations  17.6 us (3%)
    psum x1, waiting for transfers between devices, body(): first_full = -lax.psum(first_terms, 'prow')  133 us
    reduce_scatter x1, waiting for transfers between devices, side_by_side(): lax.psum_scatter(both, axis, scatter_dimension=dim, tiled=True)  97.9 us
    reduce_scatter x1, waiting for transfers between devices, body(): lax.psum_scatter(pivot_terms, 'pcol', scatter_dimension=0, tiled=True)  57.6 us
    all_to_all x1, waiting for transfers between devices, gather_over(): return jnp.concatenate(lax.all_to_all(repeated, name, 0, 0), axis=dim)  49.2 us
    all_to_all x2, waiting for transfers between devices, sent_to_all(): return lax.all_to_all(copies, axis, split_axis=0, concat_axis=0, tiled=True)  45.2 us
    psum x1, waiting for transfers between devices, body(): second_full = -lax.psum(second_terms, 'prow')  23.9 us
    dot_general x4, matrix products, batched(): jnp.einsum('kab,kbd->kad', left, right, precision=lax.Precision.HIGHEST)  20.6 us
    dot_general x4, matrix products, batched_left_t(): jnp.einsum('kba,kbd->kad', left, right, precision=lax.Precision.HIGHEST)  20.2 us
  transfers between devices with their start and end apart: 8, of which 7 were waited for; matrix products, arithmetic and copies ran while one was open for 15% of the time, Pallas kernels for 0%

profile of v1, /device:TPU:1, one launch (start us, length us, event | category | flops | bytes accessed | tf_op | source)
XLA Modules:
  0.0 608.6 jit_solution(18038225165876086862)
XLA Ops:
  8.0 3.3 stack.2
  11.3 8.6 %all-to-all-start = ((f32[16,1,256,256]{3,2,1,0:T(8,128)}), f32[16,1,256,256]{3,2,1,0:T(8,128)}, u32[]{:S(2)}, u32[]{:S(2)}) async-start(f32[16,1,256,256]{3,2,1,0:T(8,128)} %stack.2), calls=%async_computation | async-start | bytes 8388608 | tf_op jit(solution)/shard_map/all_to_all | solution.py:9
  20.6 2.8 gather_fusion.3
  23.4 49.2 %all-to-all-done = f32[16,1,256,256]{3,2,1,0:T(8,128)} async-done(((f32[16,1,256,256]{3,2,1,0:T(8,128)}), f32[16,1,256,256]{3,2,1,0:T(8,128)}, u32[]{:S(2)}, u32[]{:S(2)}) %all-to-all-start) | async-done | bytes 4194336 | tf_op jit(solution)/shard_map/all_to_all | solution.py:9
  72.6 9.7 %fusion.2 = f32[16,256,256]{2,1,0:T(8,128)} fusion(f32[16,256,256]{2,1,0:T(8,128)} %gather_fusion.3, pred[16]{0:T(512)(128)(4,1)S(1)} %compare_and_fusion.4, f32[16,1,256,256]{3,2,1,0:T(8,128)} %all-to-all-done), kind=kOutput, calls=%fused_computation.18 | convolution fusion | flops 3222274048 | bytes 12582928 | tf_op jit(solution)/shard_map/kab,kbd->kad/dot_general | solution.py:47
  86.7 4.2 gather_fusion.5
  90.9 132.7 %all-reduce.3.cloned.1.call-done = f32[16,256,256]{2,1,0:T(8,128)} async-done(((f32[16,256,256]{2,1,0:T(8,128)}), f32[16,256,256]{2,1,0:T(8,128)}) %all-reduce.3.cloned.1.call-update) | async-done | bytes 4194320 | tf_op jit(solution)/shard_map/psum | solution.py:94
  223.6 4.5 neg.15
  228.1 4.2 gather_fusion.6
  232.3 6.1 fusion.17
  240.8 4.4 scatter_fusion
  251.9 6.8 %fusion.68 = (f32[16,256,256]{2,1,0:T(8,128)}, f32[16,256,256]{2,1,0:T(8,128)S(1)}) fusion(f32[16,512,256]{2,1,0:T(8,128)} %all-gather.2.cloned.1.call-done), kind=kLoop, calls=%fused_computation.118 | loop fusion | bytes 16777216 | tf_op jit(solution)/shard_map/split | solution.py:16
  261.3 5.6 fusion
  269.5 57.6 %reduce-scatter.3.cloned.1.call-done = f32[1,256,256]{2,1,0:T(8,128)} async-done(((f32[16,256,256]{2,1,0:T(8,128)}), f32[1,256,256]{2,1,0:T(8,128)}) %reduce-scatter.3.cloned.1.call-update) | async-done | bytes 262160 | tf_op jit(solution)/shard_map/reduce_scatter | solution.py:109
  329.7 8.3 %all-to-all-start.1 = ((f32[8,1,256,256]{3,2,1,0:T(8,128)}), f32[8,1,256,256]{3,2,1,0:T(8,128)}, u32[]{:S(2)}, u32[]{:S(2)}) async-start(f32[8,1,256,256]{3,2,1,0:T(8,128)} %broadcast_in_dim.110), calls=%async_computation.2 | async-start | bytes 4194304 | tf_op jit(solution)/shard_map/all_to_all | solution.py:21
  337.9 10.9 %reduce-scatter.5.cloned.1.call-start = ((), (), s32[]{:S(2)}) async-start(), calls=%async_computation.9 | async-start | bytes 8912896 | tf_op jit(solution)/shard_map/reduce_scatter | solution.py:30
  355.9 4.2 gather_fusion.9
  360.1 2.9 gather_fusion.10
  363.0 6.8 %fusion.22 = f32[8,256,256]{2,1,0:T(8,128)} fusion(f32[8,256,256]{2,1,0:T(8,128)S(1)} %gather_fusion.10, f32[8,256,256]{2,1,0:T(8,128)} %gather_fusion.9, f32[8]{0:T(128)S(1)} %get-tuple-element.106, pred[8]{0:T(512)(128)(4,1)S(1)} %get-tuple-element.93, pred[8]{0:T(512)(128)(4,1)S(1)} %get-tuple-element.91), kind=kOutput, calls=%fused_computation.34 | convolution fusion | flops 1612185600 | bytes 6291504 | tf_op jit(solution)/shard_map/kba,kbd->kad/dot_general | solution.py:51
  372.2 5.1 scatter_fusion.1
  379.5 2.8 fusion.36
  382.2 23.9 %all-reduce.5.cloned.1.call-done = f32[16,256,256]{2,1,0:T(8,128)} async-done(((f32[16,256,256]{2,1,0:T(8,128)}), f32[16,256,256]{2,1,0:T(8,128)}) %all-reduce.5.cloned.1.call-update) | async-done | bytes 4194320 | tf_op jit(solution)/shard_map/psum | solution.py:103
  406.1 4.5 neg.16
  410.6 4.2 gather_fusion.11
  414.8 6.8 %fusion.27 = f32[8,256,256]{2,1,0:T(8,128)} fusion(f32[8,256,256]{2,1,0:T(8,128)} %gather_fusion.11, f32[8,256,256]{2,1,0:T(8,128)S(1)} %gather_fusion.10, f32[8]{0:T(128)S(1)} %get-tuple-element.106, pred[8]{0:T(512)(128)(4,1)S(1)} %get-tuple-element.93), kind=kOutput, calls=%fused_computation.35 | convolution fusion | flops 1612185600 | bytes 6291496 | tf_op jit(solution)/shard_map/kba,kbd->kad/dot_general | solution.py:51
  424.0 4.4 scatter_fusion.2
  428.3 7.4 %pad_maximum_fusion = f32[16,512,256]{2,1,0:T(8,128)} fusion(f32[16,256,256]{2,1,0:T(8,128)} %scatter_fusion.2, f32[16,256,256]{2,1,0:T(8,128)} %fusion.36), kind=kLoop, calls=%fused_computation.15 | loop fusion | flops 2097152 | bytes 16777216 | tf_op jit(solution)/shard_map/concatenate | solution.py:29
  435.8 97.9 %reduce-scatter.5.cloned.1.call-done = f32[1,512,256]{2,1,0:T(8,128)} async-done(((f32[16,512,256]{2,1,0:T(8,128)}), f32[1,512,256]{2,1,0:T(8,128)}) %reduce-scatter.5.cloned.1.call-update) | async-done | bytes 524304 | tf_op jit(solution)/shard_map/reduce_scatter | solution.py:30
  535.1 4.1 broadcast_in_dim.125
  539.2 4.9 all-to-all-start.2
  548.0 44.9 %all-to-all-done.2 = f32[8,1,131072]{2,1,0:T(1,128)} async-done(((f32[8,1,131072]{2,1,0:T(1,128)}), f32[8,1,131072]{2,1,0:T(1,128)}, u32[]{:S(2)}, u32[]{:S(2)}) %all-to-all-start.2) | async-done | bytes 4194336 | tf_op jit(solution)/shard_map/all_to_all | solution.py:21
  592.9 5.3 reduce_sum.22
  (100 shorter events, 42.3 us)
Async XLA Ops:
  11.3 8.6 %copy-start.11 = (s32[16,8]{0,1:T(8,128)S(1)}, s32[16,8]{0,1:T(8,128)}, u32[]{:S(2)}) copy-start(s32[16,8]{0,1:T(8,128)} %param.17) | copy-start | bytes 1540
  11.3 8.7 %copy-start.7 = (f32[256,512]{1,0:T(8,128)S(1)}, f32[256,512]{1,0:T(8,128)}, u32[]{:S(2)}) copy-start(f32[256,512]{1,0:T(8,128)} %param.16) | copy-start | bytes 1572868
  11.3 9.3 %copy-start = (s32[16]{0:T(128)S(1)}, s32[16]{0:T(128)}, u32[]{:S(2)}) copy-start(s32[16]{0:T(128)} %param.18) | copy-start | bytes 196
  11.3 61.3 %all-to-all-start = ((f32[16,1,256,256]{3,2,1,0:T(8,128)}), f32[16,1,256,256]{3,2,1,0:T(8,128)}, u32[]{:S(2)}, u32[]{:S(2)}) async-start(f32[16,1,256,256]{3,2,1,0:T(8,128)} %stack.2), calls=%async_computation | async-start | bytes 8388608 | tf_op jit(solution)/shard_map/all_to_all | solution.py:9
  19.9 203.7 %all-reduce.3.cloned.1.call-start = ((), (), s32[]{:S(2)}) async-start(), calls=%async_computation.5 | async-start | bytes 8388608 | tf_op jit(solution)/shard_map/psum | solution.py:94
  82.3 0.9 copy-start.6
  82.3 1.0 copy-start.10
  82.3 169.6 %all-gather.2.cloned.1.call-start = ((), (), s32[]{:S(2)}) async-start(), calls=%async_computation.7 | async-start | bytes 8912896 | tf_op jit(solution)/shard_map/all_gather | solution.py:15
  84.2 243.0 %reduce-scatter.3.cloned.1.call-start = ((), (), s32[]{:S(2)}) async-start(), calls=%async_computation.6 | async-start | bytes 4456448 | tf_op jit(solution)/shard_map/reduce_scatter | solution.py:109
  245.2 160.9 %all-reduce.5.cloned.1.call-start = ((), (), s32[]{:S(2)}) async-start(), calls=%async_computation.8 | async-start | bytes 8388608 | tf_op jit(solution)/shard_map/psum | solution.py:103
  251.9 8.0 %copy-start.1 = (f32[16,512,256]{2,1,0:T(8,128)S(1)}, f32[16,512,256]{2,1,0:T(8,128)}, u32[]{:S(2)}) copy-start(f32[16,512,256]{2,1,0:T(8,128)} %all-gather.2.cloned.1.call-done) | copy-start | bytes 25165828
  251.9 9.4 %copy-start.2 = (f32[16,256,256]{2,1,0:T(8,128)S(1)}, f32[16,256,256]{2,1,0:T(8,128)}, u32[]{:S(2)}) copy-start(f32[16,256,256]{2,1,0:T(8,128)} %gather_fusion.7) | copy-start | bytes 12582916
  261.3 5.6 copy-start.4
  269.5 85.7 %copy-start.12 = (s32[3]{0:T(128)S(1)}, s32[3]{0:T(128)}, u32[]{:S(2)}) copy-start(s32[3]{0:T(128)} %constant.173.clone.1) | copy-start | bytes 40
  329.7 47.9 %all-to-all-start.1 = ((f32[8,1,256,256]{3,2,1,0:T(8,128)}), f32[8,1,256,256]{3,2,1,0:T(8,128)}, u32[]{:S(2)}, u32[]{:S(2)}) async-start(f32[8,1,256,256]{3,2,1,0:T(8,128)} %broadcast_in_dim.110), calls=%async_computation.2 | async-start | bytes 4194304 | tf_op jit(solution)/shard_map/all_to_all | solution.py:21
  337.9 195.7 %reduce-scatter.5.cloned.1.call-start = ((), (), s32[]{:S(2)}) async-start(), calls=%async_computation.9 | async-start | bytes 8912896 | tf_op jit(solution)/shard_map/reduce_scatter | solution.py:30
  372.2 7.2 %copy-start.8 = (f32[1,256,256]{2,1,0:T(8,128)S(1)}, f32[1,256,256]{2,1,0:T(8,128)}, u32[]{:S(2)}) copy-start(f32[1,256,256]{2,1,0:T(8,128)} %param.20) | copy-start | bytes 786436
  379.4 31.2 %copy-start.5 = (f32[1,256,256]{2,1,0:T(8,128)}, f32[1,256,256]{2,1,0:T(8,128)S(1)}, u32[]{:S(2)}) copy-start(f32[1,256,256]{2,1,0:T(8,128)S(1)} %bitcast_subtract_fusion) | copy-start | bytes 786436
  421.6 2.4 copy-start.3
  539.2 4.9 copy-start.9
  539.2 53.7 %all-to-all-start.2 = ((f32[8,1,131072]{2,1,0:T(1,128)}), f32[8,1,131072]{2,1,0:T(1,128)}, u32[]{:S(2)}, u32[]{:S(2)}) async-start(f32[8,1,131072]{2,1,0:T(1,128)} %broadcast_in_dim.125), calls=%async_computation.4 | async-start | bytes 8388608 | tf_op jit(solution)/shard_map/all_to_all | solution.py:21
Sparse Core Ops, SparseCore 0:
  82.4 141.1 all-reduce.2
  269.6 136.4 all-reduce.4
Sparse Core Ops, SparseCore 1:
  85.8 84.5 all-gather.1
  245.3 81.8 reduce-scatter.2
  435.9 97.8 reduce-scatter.4
